TPU v7x, 32 devices: a whole 2x2x4 slice. The times are simulated.
32 devices in a mesh: dp: 16 (over z, x, core), seq: 2 (over y).
Axes of the slice: x: 2, y: 2, z: 4, core: 2. Of those that a mesh axis runs over, the one named last changes fastest.
Arguments:
- gene_ids: int32 [16, 2048], P('dp', 'seq'), may hold values from 0 to 9215, as said below
- homolog_ids: int32 [16, 2048], P('dp', 'seq'), may hold values from 0 to 9215, as said below
- knowledge_ids: int32 [16, 2048], P('dp', 'seq'), may hold values from 0 to 9215, as said below
- expr_bins: int32 [16, 2048], P('dp', 'seq'), may hold values from 0 to 127
- species: int32 [16], P('dp'), may hold values from 0 to 1, as said below
- cell_lengths: int32 [16], P('dp'), may hold values from 1025 to 2048, as said below
- gene_table: bfloat16 [9216, 768], P(('dp', 'seq')), may hold values from -4.1875 to 4.1875
- knowledge_tables: bfloat16 [4, 9216, 768], P(None, ('dp', 'seq')), may hold values from -2.09375 to 2.09375
- expr_table: bfloat16 [128, 768], replicated, may hold values from -4.1875 to 4.1875
- w_query: bfloat16 [768, 768], replicated, may hold values from -0.21875 to 0.21875
- b_query: float32 [768], replicated, may hold values from -1.8 to 1.8
- w_key: bfloat16 [768, 768], replicated, may hold values from -0.21875 to 0.21875
- w_value: bfloat16 [768, 768], replicated, may hold values from -0.21875 to 0.21875
- b_value: float32 [768], replicated, may hold values from -1.8 to 1.8
- w_out: bfloat16 [768, 768], replicated, may hold values from -2.5 to 2.5
- b_out: float32 [768], replicated, may hold values from -1.8 to 1.8
- gain_one: float32 [768], replicated, may hold values from 0.1 to 1.9
- shift_one: float32 [768], replicated, may hold values from -1.8 to 1.8
- w_up: bfloat16 [768, 3072], replicated, may hold values from -0.21875 to 0.21875
- b_up: float32 [3072], replicated, may hold values from -1.8 to 1.8
- w_down: bfloat16 [3072, 768], replicated, may hold values from -0.109375 to 0.109375
- b_down: float32 [768], replicated, may hold values from -1.8 to 1.8
- gain_two: float32 [768], replicated, may hold values from 0.1 to 1.9
- shift_two: float32 [768], replicated, may hold values from -1.8 to 1.8
- cotangent: bfloat16 [16, 2048, 768], P('dp', 'seq'), may hold values from -6 to 6
Outputs:
- layer_output: bfloat16 [16, 2048, 768], P('dp', 'seq')
- gene_table_grad: float32 [9216, 768], P(('dp', 'seq'))
- knowledge_grad: float32 [9216, 768], P(('dp', 'seq'))
- expr_table_grad: float32 [128, 768], replicated
- w_query_grad: float32 [768, 768], replicated
- b_query_grad: float32 [768], replicated
- w_key_grad: float32 [768, 768], replicated
- w_value_grad: float32 [768, 768], replicated
- b_value_grad: float32 [768], replicated
- w_out_grad: float32 [768, 768], replicated
- b_out_grad: float32 [768], replicated
- gain_one_grad: float32 [768], replicated
- shift_one_grad: float32 [768], replicated
- w_up_grad: float32 [768, 3072], replicated
- b_up_grad: float32 [3072], replicated
- w_down_grad: float32 [3072, 768], replicated
- b_down_grad: float32 [768], replicated
- gain_two_grad: float32 [768], replicated
- shift_two_grad: float32 [768], replicated
- row_counts: int32 [2, 9216], P(None, ('dp', 'seq'))
Inputs may be any that keep to these rules, and one draw needn't show every extreme that they name: Of the 1024 genes that one device holds (the cells of its dp index, the positions of its seq index), at most 64 have an id in one block of 288 rows (ids r * 288 to (r + 1) * 288 - 1); in every draw one block has exactly 64 from every device. A gene's gene_ids and homolog_ids lie in the same block. `homolog_ids`: as gene_ids: at most 64 of one device's genes in one block of 288 rows, one block reaching 64 from every device, and the same block as gene_ids for every gene. `knowledge_ids`: at most 64 of one device's genes in one block of 288 rows; in every draw one block has exactly 64 from every device. `species`: exactly a quarter of the cells, rounded down and at least one, have 1. `cell_lengths`: one cell has 2048 and one has 1025.
All inputs are finite; a program needn't handle non-finite values.
Results may differ from a plain program's by a relative error of at most 0.015.
The roundings to bfloat16 on the way count: a program that leaves them out, or rounds other values in their place, can miss the bound.
Values may be sent and summed in bfloat16 or wider, within the bound.
No kernel may reach another device: no remote copies, remote signals or barrier semaphores. Data moves between devices by JAX's collectives and lax.ppermute only.
A program may use at most 192 MiB of HBM per device.

v0:
```python
import jax
import jax.numpy as jnp
from jax import lax
from jax.sharding import PartitionSpec as P

HEADS = 12
HEAD_DIM = 64


def layer_norm(value, gain_vec, shift_vec):
    centre = jnp.mean(value, axis=-1, keepdims=True)
    centred = value - centre
    variance = jnp.mean(centred * centred, axis=-1, keepdims=True)
    return centred * lax.rsqrt(variance + 1e-05) * gain_vec + shift_vec


def gelu_exact(value):
    return jax.nn.gelu(value, approximate=False)


def head_split(array):
    return array.reshape(array.shape[0], HEADS, HEAD_DIM).transpose(1, 0, 2)


def head_merge(array):
    return array.transpose(1, 0, 2).reshape(array.shape[1], HEADS * HEAD_DIM)


def head_scores(query_head, key_head, valid_keys):
    scores = jnp.dot(query_head, key_head.T, preferred_element_type=jnp.float32) * HEAD_DIM ** (
        -0.5
    )
    return jnp.where(valid_keys[None, :], scores, -1e30)


def attend_forward(query_cell, key_cell, value_cell, valid_keys):

    def one_head(head_parts):
        query_head, key_head, value_head = head_parts
        scores = head_scores(query_head, key_head, valid_keys)
        log_total = jax.nn.logsumexp(scores, axis=-1, keepdims=True)
        probs_low = jnp.exp(scores - log_total).astype(jnp.bfloat16)
        context = jnp.dot(probs_low, value_head, preferred_element_type=jnp.float32)
        return (context, log_total[:, 0])

    context, log_total = lax.map(
        one_head, (head_split(query_cell), head_split(key_cell), head_split(value_cell))
    )
    return (head_merge(context), log_total)


def attend_backward(query_cell, key_cell, value_cell, valid_keys, log_total, grad_context):

    def one_head(head_parts):
        query_head, key_head, value_head, total_head, grad_head = head_parts
        scores = head_scores(query_head, key_head, valid_keys)
        attn_probs = jnp.exp(scores - total_head[:, None])
        probs_low = attn_probs.astype(jnp.bfloat16)
        grad_probs = jnp.dot(grad_head, value_head.T, preferred_element_type=jnp.float32)
        inner = jnp.sum(attn_probs * grad_probs, axis=-1, keepdims=True)
        grad_scores = (attn_probs * (grad_probs - inner) * HEAD_DIM ** (-0.5)).astype(jnp.bfloat16)
        grad_query = jnp.dot(grad_scores, key_head, preferred_element_type=jnp.float32)
        grad_key = jnp.dot(grad_scores.T, query_head, preferred_element_type=jnp.float32)
        grad_value = jnp.dot(probs_low.T, grad_head, preferred_element_type=jnp.float32)
        return (grad_query, grad_key, grad_value)

    grad_query, grad_key, grad_value = lax.map(
        one_head,
        (
            head_split(query_cell),
            head_split(key_cell),
            head_split(value_cell),
            log_total,
            head_split(grad_context),
        ),
    )
    return (head_merge(grad_query), head_merge(grad_key), head_merge(grad_value))


def place(identity, rows_dev, devices):
    owner_dev = identity // rows_dev
    owner_hits = (owner_dev[:, None] == jnp.arange(devices)[None, :]).astype(jnp.int32)
    before = jnp.cumsum(owner_hits, axis=0) - owner_hits
    slot_rank = jnp.sum(before * owner_hits, axis=1)
    return (owner_dev, slot_rank, identity - owner_dev * rows_dev)


def local(
    gene_ids,
    homolog_ids,
    knowledge_ids,
    expr_bins,
    species,
    cell_lengths,
    gene_table,
    knowledge_tables,
    expr_table,
    w_query,
    b_query,
    w_key,
    w_value,
    b_value,
    w_out,
    b_out,
    gain_one,
    shift_one,
    w_up,
    b_up,
    w_down,
    b_down,
    gain_two,
    shift_two,
    cotangent,
):
    cells_here, half_len = gene_ids.shape
    width = gene_table.shape[1]
    rows_dev = gene_table.shape[0]
    devices = lax.axis_size(("dp", "seq"))
    looked = cells_here * half_len
    capacity = 2 * looked // devices
    slots_all = 2 * capacity
    chosen = jnp.where(species[:, None] == 1, homolog_ids, gene_ids).reshape(-1)
    gene_owner, gene_rank, gene_local = place(chosen, rows_dev, devices)
    know_owner, know_rank, know_local = place(knowledge_ids.reshape(-1), rows_dev, devices)
    gene_slot = gene_owner * slots_all + gene_rank
    know_slot = know_owner * slots_all + capacity + know_rank
    requests = jnp.full((devices * slots_all,), -1, jnp.int32)
    requests = requests.at[gene_slot].set(gene_local).at[know_slot].set(know_local + rows_dev)
    requests = requests.reshape(devices, slots_all)
    know_sum = jnp.sum(knowledge_tables.astype(jnp.float32), axis=0).astype(jnp.bfloat16)
    combined = jnp.concatenate([gene_table, know_sum], axis=0)
    received = lax.all_to_all(requests, ("dp", "seq"), split_axis=0, concat_axis=0, tiled=True)
    found = jnp.take(combined, jnp.clip(received, 0, 2 * rows_dev - 1), axis=0)
    fetched = lax.all_to_all(found, ("dp", "seq"), split_axis=0, concat_axis=0, tiled=True)
    fetched_flat = fetched.reshape(devices * slots_all, width)
    bin_hot = expr_bins.reshape(-1)[:, None] == jnp.arange(expr_table.shape[0])[None, :]
    expr_rows = jnp.dot(
        bin_hot.astype(jnp.bfloat16), expr_table, preferred_element_type=jnp.float32
    )
    embedded = (
        fetched_flat[gene_slot].astype(jnp.float32)
        + fetched_flat[know_slot].astype(jnp.float32)
        + expr_rows
    )
    x_low = embedded.astype(jnp.bfloat16)
    query_all = (jnp.dot(x_low, w_query, preferred_element_type=jnp.float32) + b_query).astype(
        jnp.bfloat16
    )
    key_local = jnp.dot(x_low, w_key, preferred_element_type=jnp.float32).astype(jnp.bfloat16)
    value_local = (jnp.dot(x_low, w_value, preferred_element_type=jnp.float32) + b_value).astype(
        jnp.bfloat16
    )
    query_cells = query_all.reshape(cells_here, half_len, width)
    key_cells = key_local.reshape(cells_here, half_len, width)
    value_cells = value_local.reshape(cells_here, half_len, width)
    key_whole, value_whole = (
        lax.all_gather(key_cells, "seq", axis=1, tiled=True),
        lax.all_gather(value_cells, "seq", axis=1, tiled=True),
    )
    positions = jnp.arange(key_whole.shape[1])
    valid_keys = positions[None, :] < cell_lengths[:, None]
    context_cells, log_totals = lax.map(
        lambda cell_parts: attend_forward(*cell_parts),
        (query_cells, key_whole, value_whole, valid_keys),
    )
    context_low = context_cells.reshape(looked, width).astype(jnp.bfloat16)
    attn_out = jnp.dot(context_low, w_out, preferred_element_type=jnp.float32) + b_out
    normed_one, norm_one_back = jax.vjp(layer_norm, embedded + attn_out, gain_one, shift_one)
    normed_low = normed_one.astype(jnp.bfloat16)
    pre_ffn = jnp.dot(normed_low, w_up, preferred_element_type=jnp.float32) + b_up
    gelu_value, gelu_back = jax.vjp(gelu_exact, pre_ffn)
    activated = gelu_value.astype(jnp.bfloat16)
    ffn_out = jnp.dot(activated, w_down, preferred_element_type=jnp.float32) + b_down
    final, norm_two_back = jax.vjp(layer_norm, normed_one + ffn_out, gain_two, shift_two)
    layer_output = final.astype(jnp.bfloat16).reshape(cells_here, half_len, width)
    grad_final = cotangent.reshape(looked, width).astype(jnp.float32)
    grad_two, gain_two_grad, shift_two_grad = norm_two_back(grad_final)
    grad_ffn_low = grad_two.astype(jnp.bfloat16)
    w_down_grad = jnp.einsum(
        "tf,td->fd", activated, grad_ffn_low, preferred_element_type=jnp.float32
    )
    b_down_grad = jnp.sum(grad_ffn_low.astype(jnp.float32), axis=0)
    grad_act = jnp.einsum("td,fd->tf", grad_ffn_low, w_down, preferred_element_type=jnp.float32)
    grad_pre_low = gelu_back(grad_act)[0].astype(jnp.bfloat16)
    w_up_grad = jnp.einsum(
        "td,tf->df", normed_low, grad_pre_low, preferred_element_type=jnp.float32
    )
    b_up_grad = jnp.sum(grad_pre_low.astype(jnp.float32), axis=0)
    grad_normed = grad_two + jnp.einsum(
        "tf,df->td", grad_pre_low, w_up, preferred_element_type=jnp.float32
    )
    grad_one, gain_one_grad, shift_one_grad = norm_one_back(grad_normed)
    grad_attn_low = grad_one.astype(jnp.bfloat16)
    w_out_grad = jnp.einsum(
        "te,td->ed", context_low, grad_attn_low, preferred_element_type=jnp.float32
    )
    b_out_grad = jnp.sum(grad_attn_low.astype(jnp.float32), axis=0)
    grad_context = jnp.einsum(
        "td,ed->te", grad_attn_low, w_out, preferred_element_type=jnp.float32
    ).astype(jnp.bfloat16)
    key_back, value_back = (key_whole, value_whole)
    grad_q_cells, grad_k_whole, grad_v_whole = lax.map(
        lambda cell_parts: attend_backward(*cell_parts),
        (
            query_cells,
            key_back,
            value_back,
            valid_keys,
            log_totals,
            grad_context.reshape(cells_here, half_len, width),
        ),
    )
    grad_key_part, grad_value_part = (
        lax.psum_scatter(grad_k_whole, "seq", scatter_dimension=1, tiled=True),
        lax.psum_scatter(grad_v_whole, "seq", scatter_dimension=1, tiled=True),
    )
    grad_query_low = grad_q_cells.reshape(looked, width).astype(jnp.bfloat16)
    grad_key_low = grad_key_part.reshape(looked, width).astype(jnp.bfloat16)
    grad_value_low = grad_value_part.reshape(looked, width).astype(jnp.bfloat16)
    w_query_grad = jnp.einsum(
        "td,te->de", x_low, grad_query_low, preferred_element_type=jnp.float32
    )
    b_query_grad = jnp.sum(grad_query_low.astype(jnp.float32), axis=0)
    w_key_grad = jnp.einsum("td,te->de", x_low, grad_key_low, preferred_element_type=jnp.float32)
    w_value_grad = jnp.einsum(
        "td,te->de", x_low, grad_value_low, preferred_element_type=jnp.float32
    )
    b_value_grad = jnp.sum(grad_value_low.astype(jnp.float32), axis=0)
    grad_embedded = (
        grad_one
        + jnp.einsum("te,de->td", grad_query_low, w_query, preferred_element_type=jnp.float32)
        + jnp.einsum("te,de->td", grad_key_low, w_key, preferred_element_type=jnp.float32)
        + jnp.einsum("te,de->td", grad_value_low, w_value, preferred_element_type=jnp.float32)
    )
    expr_grad_local = jnp.dot(
        bin_hot.astype(jnp.float32).T, grad_embedded, precision=lax.Precision.HIGHEST
    )
    outgoing = jnp.zeros((devices * slots_all, width), jnp.float32)
    outgoing = outgoing.at[gene_slot].set(grad_embedded).at[know_slot].set(grad_embedded)
    outgoing = outgoing.reshape(devices, slots_all, width)
    returned = lax.all_to_all(
        outgoing.astype(jnp.bfloat16), ("dp", "seq"), split_axis=0, concat_axis=0, tiled=True
    ).astype(outgoing.dtype)
    owned = jnp.arange(2 * rows_dev)[:, None] == received.reshape(1, -1)
    table_grads = jnp.dot(
        owned.astype(jnp.float32),
        returned.reshape(devices * slots_all, width),
        precision=lax.Precision.HIGHEST,
    )
    row_counts = jnp.sum(owned.astype(jnp.int32), axis=1).reshape(2, rows_dev)
    whole_summed = lax.psum(
        (
            expr_grad_local,
            w_query_grad,
            b_query_grad,
            w_key_grad,
            w_value_grad,
            b_value_grad,
            w_out_grad,
            b_out_grad,
            gain_one_grad,
            shift_one_grad,
            w_down_grad,
            b_down_grad,
            gain_two_grad,
            shift_two_grad,
            w_up_grad,
            b_up_grad,
        ),
        ("dp", "seq"),
    )
    rest_summed = whole_summed[:10]
    ffn_summed = whole_summed[10:]
    return (
        layer_output,
        table_grads[:rows_dev],
        table_grads[rows_dev:],
        rest_summed[0],
        rest_summed[1],
        rest_summed[2],
        rest_summed[3],
        rest_summed[4],
        rest_summed[5],
        rest_summed[6],
        rest_summed[7],
        rest_summed[8],
        rest_summed[9],
        ffn_summed[4],
        ffn_summed[5],
        ffn_summed[0],
        ffn_summed[1],
        ffn_summed[2],
        ffn_summed[3],
        row_counts,
    )


def solution(mesh):
    placed = (
        P("dp", "seq"),
        P("dp", "seq"),
        P("dp", "seq"),
        P("dp", "seq"),
        P("dp"),
        P("dp"),
        P(("dp", "seq"), None),
        P(None, ("dp", "seq"), None),
        P(),
        P(),
        P(),
        P(),
        P(),
        P(),
        P(),
        P(),
        P(),
        P(),
        P(),
        P(),
        P(),
        P(),
        P(),
        P(),
        P("dp", "seq", None),
    )
    return jax.shard_map(
        local,
        mesh=mesh,
        in_specs=placed,
        out_specs=(
            P("dp", "seq", None),
            P(("dp", "seq"), None),
            P(("dp", "seq"), None),
            P(),
            P(),
            P(),
            P(),
            P(),
            P(),
            P(),
            P(),
            P(),
            P(),
            P(),
            P(),
            P(),
            P(),
            P(),
            P(),
            P(None, ("dp", "seq")),
        ),
        check_vma=False,
    )
```

profile of v0, /device:TPU:0, one launch (start us, length us, event | category | flops | bytes accessed | tf_op | source)
XLA Modules:
  0.0 1586.1 jit_solution(10476663562340610577)
XLA Ops:
  10.3 9.0 reduce-window.14
  19.3 9.0 reduce-window.16
  40.6 7.3 all-to-all-start
  55.1 17.7 %gather_fusion = bf16[4096,768]{1,0:T(8,128)(2,1)} fusion(bf16[576,768]{1,0:T(8,128)(2,1)S(1)} %pad_maximum_fusion, s32[4096]{0:T(1024)S(1)} %fusion.98), kind=kCustom, calls=%fused_computation | custom fusion | bytes 12599296 | tf_op jit(solution)/shard_map/jit(_take)/gather | solution.py:133
  83.1 140.1 %all-to-all-done.1 = bf16[32,128,768]{2,1,0:T(8,128)(2,1)} async-done(((bf16[32,128,768]{2,1,0:T(8,128)(2,1)}), bf16[32,128,768]{2,1,0:T(8,128)(2,1)}, u32[]{:S(2)}, u32[]{:S(2)}) %all-to-all-start.1) | async-done | bytes 6291488 | tf_op jit(solution)/shard_map/all_to_all | solution.py:134
  223.3 9.2 gather_fusion.2
  232.4 9.2 gather_fusion.1
  269.0 28.5 %all-gather.5.cloned.1.call-done = bf16[2048,768]{1,0:T(8,128)(2,1)} async-done(((bf16[1024,768]{1,0:T(8,128)(2,1)}), bf16[2048,768]{1,0:T(8,128)(2,1)}) %all-gather.5.cloned.1.call-update) | async-done | bytes 3145744 | tf_op jit(solution)/shard_map/all_gather | solution.py:157
  308.9 35.7 %all-gather.7.cloned.1.call-done = bf16[2048,768]{1,0:T(8,128)(2,1)} async-done(((bf16[1024,768]{1,0:T(8,128)(2,1)}), bf16[2048,768]{1,0:T(8,128)(2,1)}) %all-gather.7.cloned.1.call-update) | async-done | bytes 3145744 | tf_op jit(solution)/shard_map/all_gather | solution.py:158
  356.0 117.5 %while.48 = (s32[]{:T(128)}, bf16[12,1024,64]{1,2,0:T(8,128)(2,1)S(1)}, f32[12,1024]{1,0:T(8,128)}, bf16[12,1024,64]{2,1,0:T(8,128)(2,1)}, bf16[12,2048,64]{2,1,...) while((s32[]{:T(128)}, ...), condition=%wide.region_12.13_spmd.clone, body=%wide.region_9.12_spmd.clone.sunk | while | flops 559948800 | bytes 26810476 | solution.py:46
  478.6 48.7 %multiply_convert_fusion.1 = (bf16[1024,3072]{1,0:T(8,128)(2,1)S(1)}, f32[1024,3072]{1,0:T(8,128)}, f32[1024,3072]{1,0:T(8,128)}) fusion(f32[3072]{0:T(1024)S(1)} %copy-done.50, bf16[768,3072]{1,0:T(8,128)(2,1)S(1)} %bitcast.320, f32[1024,768]{0,1:T(8,128)S(1)} %get-tuple-element.424, f32[768]{0:T(1024)S(1)} %copy-done.55, f32[768]{0:T(1024)S(1)} %copy-done.43, ...), kind=kOutput, calls=%fused_computation.75 | convolution fusion | flops 5043388416 | bytes 39348224 | tf_op jit(solution)/shard_map/dot_general | solution.py:170
  540.0 19.4 %convert_reduce_fusion = (f32[3072]{0:T(1024)}, bf16[1024,3072]{1,0:T(8,128)(2,1)}) fusion(f32[1024,3072]{1,0:T(8,128)} %get-tuple-element.403, bf16[1024,768]{0,1:T(8,128)(2,1)} %get-tuple-element.397, bf16[3072,768]{1,0:T(8,128)(2,1)} %param.49, f32[1024,3072]{1,0:T(8,128)} %get-tuple-element.425, f32[3072]{0:T(1024)S(1)} %copy-done.50), kind=kOutput, calls=%fused_computation.73 | convolution fusion | flops 4885312512 | bytes 37773312 | tf_op jit(solution)/shard_map/td,fd->tf/dot_general | solution.py:183
  559.4 11.4 multiply_reduce_fusion.1
  577.2 225.5 %while.49 = (s32[]{:T(128)}, bf16[12,1024,64]{1,2,0:T(8,128)(2,1)S(1)}, f32[12,2048,64]{1,2,0:T(8,128)}, f32[12,2048,64]{1,2,0:T(8,128)}, bf16[12,1024,64]{2,1,0...) while((s32[]{:T(128)}, ...), condition=%wide.region_23.24_spmd.clone, body=%wide.region_21.23_spmd.clone.sunk | while | flops 1375732736 | bytes 66888828 | solution.py:67
  813.5 8.1 fusion.112
  821.6 7.7 fusion.125
  829.3 50.7 %reduce-scatter.3.cloned.1.call-done = f32[1,1024,768]{1,2,0:T(8,128)} async-done(((f32[1,2048,768]{1,2,0:T(8,128)}), f32[1,1024,768]{1,2,0:T(8,128)}) %reduce-scatter.3.cloned.1.call-update) | async-done | bytes 3145744 | tf_op jit(solution)/shard_map/reduce_scatter | solution.py:214
  884.9 74.4 %reduce-scatter.5.cloned.1.call-done = f32[1,1024,768]{1,2,0:T(8,128)} async-done(((f32[1,2048,768]{1,2,0:T(8,128)}), f32[1,1024,768]{1,2,0:T(8,128)}) %reduce-scatter.5.cloned.1.call-update) | async-done | bytes 3145744 | tf_op jit(solution)/shard_map/reduce_scatter | solution.py:215
  978.0 11.5 scatter_custom_fusion.2
  989.5 14.9 scatter_fusion.1
  1004.4 8.0 convert_element_type.161
  1024.2 220.7 %all-reduce = (f32[768]{0:T(1024)}, f32[768]{0:T(1024)}, f32[768]{0:T(1024)}, f32[768]{0:T(1024)}, f32[768]{0:T(1024)}, /*index=5*/f32[3072]{0:T(1024)}, f32[768]{0:T(1024)}, f32[768]{0:T(1024)}, f32[768]{0:T(1024)}) all-reduce(f32[768]{0:T(1024)S(1)} %reduce_sum.262, ...), channel_id=1, replica_groups=mesh['dp'=16,'seq'=2] {'dp','seq'}, use_global_device_ids=true, to_apply=%region_31.32 | all-reduce | flops 9216 | bytes 73728 | tf_op jit(solution)/shard_map/psum | solution.py:251
  1252.6 301.8 %all-reduce.4.cloned.1.call-done = (f32[128,768]{1,0:T(8,128)}, f32[768,768]{1,0:T(8,128)}, f32[768,768]{1,0:T(8,128)}, f32[768,768]{1,0:T(8,128)}, f32[768,768]...) async-done(((f32[128,768]{1,0:T(8,128)}, f32[768,768]{1,0:T(8,128)}, f32[768,768]{1,0:T(8,128)}, f32[768,768]{1,0:T(8,128)}, f32[768,768]{1,0:T(8,128)}, ...) | async-done | bytes 28704784 | tf_op jit(solution)/shard_map/psum | solution.py:251
  1566.0 9.3 copy.175
  (442 shorter events, 516.9 us)
Async XLA Ops:
  7.2 466.4 %copy-start = (bf16[768,768]{1,0:T(8,128)(2,1)S(1)}, bf16[768,768]{1,0:T(8,128)(2,1)}, u32[]{:S(2)}) copy-start(bf16[768,768]{1,0:T(8,128)(2,1)} %param.43) | copy-start | bytes 3538948
  29.5 53.6 %copy-start.30 = (s32[1024,1]{0,1:T(1,128)}, s32[1024,1]{0,1:T(1,128)S(1)}, u32[]{:S(2)}) copy-start(s32[1024,1]{0,1:T(1,128)S(1)} %compare_select_fusion.2) | copy-start | bytes 12292
  30.0 53.1 %copy-start.40 = (s32[1024,1]{0,1:T(1,128)}, s32[1024,1]{0,1:T(1,128)S(1)}, u32[]{:S(2)}) copy-start(s32[1024,1]{0,1:T(1,128)S(1)} %compare_select_fusion.3) | copy-start | bytes 12292
  34.9 14.9 copy-start.26
  40.6 14.4 all-to-all-start
  55.0 17.8 %copy-start.28 = (s32[32,1,128]{2,1,0:T(1,128)}, s32[32,1,128]{2,1,0:T(1,128)S(1)}, u32[]{:S(2)}) copy-start(s32[32,1,128]{2,1,0:T(1,128)S(1)} %all-to-all-done) | copy-start | bytes 49156
  79.4 143.9 %all-to-all-start.1 = ((bf16[32,128,768]{2,1,0:T(8,128)(2,1)}), bf16[32,128,768]{2,1,0:T(8,128)(2,1)}, u32[]{:S(2)}, u32[]{:S(2)}) async-start(bf16[32,128,768]{2,1,0:T(8,128)(2,1)} %broadcast_select_fusion), calls=%async_computation.1 | async-start | bytes 12582912 | tf_op jit(solution)/shard_map/all_to_all | solution.py:134
  83.0 214.4 %all-gather.5.cloned.1.call-start = ((), (), s32[]{:S(2)}) async-start(), calls=%async_computation.7 | async-start | bytes 4718592 | tf_op jit(solution)/shard_map/all_gather | solution.py:157
  253.5 91.0 %all-gather.7.cloned.1.call-start = ((), (), s32[]{:S(2)}) async-start(), calls=%async_computation.8 | async-start | bytes 4718592 | tf_op jit(solution)/shard_map/all_gather | solution.py:158
  257.6 622.4 %reduce-scatter.3.cloned.1.call-start = ((), (), s32[]{:S(2)}) async-start(), calls=%async_computation.5 | async-start | bytes 9437184 | tf_op jit(solution)/shard_map/reduce_scatter | solution.py:214
  356.0 117.6 %copy-start.53 = (f32[768]{0:T(1024)S(1)}, f32[768]{0:T(1024)}, u32[]{:S(2)}) copy-start(f32[768]{0:T(1024)} %param.44) | copy-start | bytes 9220
  473.6 53.7 %slice-start.3 = ((s8[4718592]{0:T(1024)(128)(4,1)}), s8[4194304]{0:T(1024)(128)(4,1)S(1)}, s32[]{:S(2)}) async-start(s8[4718592]{0:T(1024)(128)(4,1)} %bitcast.317), calls=%async_computation.13 | async-start | bytes 8388608
  477.7 49.6 %copy-start.7 = (f32[1024,768]{0,1:T(8,128)}, f32[1024,768]{0,1:T(8,128)S(1)}, u32[]{:S(2)}) copy-start(f32[1024,768]{0,1:T(8,128)S(1)} %get-tuple-element.424) | copy-start | bytes 9437188
  478.6 48.8 %slice-start.4 = ((s8[4718592]{0:T(1024)(128)(4,1)}), s8[524288]{0:T(1024)(128)(4,1)S(1)}, s32[]{:S(2)}) async-start(s8[4718592]{0:T(1024)(128)(4,1)} %bitcast.317), calls=%async_computation.14 | async-start | bytes 1048576
  478.6 48.8 %copy-start.54 = (f32[768]{0:T(1024)S(1)}, f32[768]{0:T(1024)}, u32[]{:S(2)}) copy-start(f32[768]{0:T(1024)} %param.50) | copy-start | bytes 9220
  559.4 11.4 copy-start.8
  802.8 156.6 %reduce-scatter.5.cloned.1.call-start = ((), (), s32[]{:S(2)}) async-start(), calls=%async_computation.6 | async-start | bytes 9437184 | tf_op jit(solution)/shard_map/reduce_scatter | solution.py:215
  803.4 751.0 %all-reduce.4.cloned.1.call-start = ((), (), s32[]{:S(2)}) async-start(), calls=%async_computation.9 | async-start | bytes 57409536 | tf_op jit(solution)/shard_map/psum | solution.py:251
  821.6 58.4 %copy-start.49 = (bf16[768,768]{1,0:T(8,128)(2,1)S(1)}, bf16[768,768]{1,0:T(8,128)(2,1)}, u32[]{:S(2)}) copy-start(bf16[768,768]{1,0:T(8,128)(2,1)} %param.40) | copy-start | bytes 3538948
  829.3 130.1 %copy-start.25 = (bf16[768,768]{1,0:T(8,128)(2,1)S(1)}, bf16[768,768]{1,0:T(8,128)(2,1)}, u32[]{:S(2)}) copy-start(bf16[768,768]{1,0:T(8,128)(2,1)} %param.41) | copy-start | bytes 3538948
  829.3 130.1 %copy-start.34 = (f32[1024]{0:T(1024)S(1)}, f32[1024]{0:T(1024)}, u32[]{:S(2)}) copy-start(f32[1024]{0:T(1024)} %copy-done.33) | copy-start | bytes 12292
  884.9 80.7 %copy-start.36 = (s32[1,1024]{1,0:T(1,128)S(1)}, s32[1,1024]{1,0:T(1,128)}, u32[]{:S(2)}) copy-start(s32[1,1024]{1,0:T(1,128)} %param.32) | copy-start | bytes 12292
  978.0 11.5 copy-start.31
  1012.5 232.4 %all-to-all-start.2 = ((bf16[32,128,768]{2,1,0:T(8,128)(2,1)}), bf16[32,128,768]{2,1,0:T(8,128)(2,1)}, u32[]{:S(2)}, u32[]{:S(2)}) async-start(bf16[32,128,768]{2,1,0:T(8,128)(2,1)} %bitcast.274), calls=%async_computation.4 | async-start | bytes 12582912 | tf_op jit(solution)/shard_map/all_to_all | solution.py:241
  (53 other events, 229.0 us)
Sparse Core Ops, SparseCore 0:
  253.7 43.7 all-gather.4
  299.6 44.9 all-gather.6
  802.9 77.0 reduce-scatter.2
  882.2 77.0 reduce-scatter.4
  974.6 579.7 all-reduce.3
where the time goes:
time: 1600 us; the launch traced here: 1590 us
  waiting for transfers between devices  637 us (40%)
  matrix products  397 us (25%)
  blocking collectives  221 us (14%)
  local copies, waits for them, and re-layouts  173 us (11%)
  other arithmetic  126 us (8%)
    psum x1, waiting for transfers between devices, local(): lax.psum((expr_grad_local, w_query_grad, b_query_grad, w_key_grad, w_valu...  302 us
    psum x1, blocking collectives, local(): lax.psum((expr_grad_local, w_query_grad, b_query_grad, w_key_grad, w_valu...  221 us
    all_to_all x1, waiting for transfers between devices, local(): lax.all_to_all(found, ('dp', 'seq'), split_axis=0, concat_axis=0, tiled=T...  140 us
    reduce_scatter x1, waiting for transfers between devices, local(): lax.psum_scatter(grad_v_whole, 'seq', scatter_dimension=1, tiled=True)  74.4 us
    dot_general x24, matrix products, head_scores(): jnp.dot(query_head, key_head.T, preferred_element_type=jnp.float32)  59.4 us
    reduce_scatter x1, waiting for transfers between devices, local(): lax.psum_scatter(grad_k_whole, 'seq', scatter_dimension=1, tiled=True)  50.7 us
    dot_general x1, matrix products, local(): jnp.dot(normed_low, w_up, preferred_element_type=jnp.float32) + b_up  48.7 us
    unnamed x149, local copies, waits for them, and re-layouts  47.2 us
  transfers between devices with their start and end apart: 8, of which 7 were waited for; matrix products, arithmetic and copies ran while one was open for 7% of the time, Pallas kernels for 0%

commit v1 on v0

--- a/solution.py
+++ b/solution.py
@@ -249,25 +249,28 @@
     )
     row_counts = jnp.sum(owned.astype(jnp.int32), axis=1).reshape(2, rows_dev)
     whole_summed = lax.psum(
-        (
-            expr_grad_local,
-            w_query_grad,
-            b_query_grad,
-            w_key_grad,
-            w_value_grad,
-            b_value_grad,
-            w_out_grad,
-            b_out_grad,
-            gain_one_grad,
-            shift_one_grad,
-            w_down_grad,
-            b_down_grad,
-            gain_two_grad,
-            shift_two_grad,
-            w_up_grad,
-            b_up_grad,
+        lax.psum(
+            (
+                expr_grad_local,
+                w_query_grad,
+                b_query_grad,
+                w_key_grad,
+                w_value_grad,
+                b_value_grad,
+                w_out_grad,
+                b_out_grad,
+                gain_one_grad,
+                shift_one_grad,
+                w_down_grad,
+                b_down_grad,
+                gain_two_grad,
+                shift_two_grad,
+                w_up_grad,
+                b_up_grad,
+            ),
+            "seq",
         ),
-        ("dp", "seq"),
+        "dp",
     )
     rest_summed = whole_summed[:10]
     ffn_summed = whole_summed[10:]

time: 1600 us -> 2300 us (1.44)
  waiting for transfers between devices: 637 us -> 1320 us
    psum x0 -> x1, waiting for transfers between devices: none -> 342 us  [local(): lax.psum(lax.psum((expr_grad_local, w_query_grad, b_query_grad, w_key_gra...]
    psum x1, waiting for transfers between devices: 302 us -> 642 us  [local(): lax.psum((expr_grad_local, w_query_grad, b_query_grad, w_key_grad, w_valu...]
    psum x0 -> x1, blocking collectives: none -> 215 us  [local(): lax.psum(lax.psum((expr_grad_local, w_query_grad, b_query_grad, w_key_gra...]
    psum x1, blocking collectives: 221 us -> 23.2 us  [local(): lax.psum((expr_grad_local, w_query_grad, b_query_grad, w_key_grad, w_valu...]
  transfers between devices with their start and end apart: 8 -> 9, of which waited for: 7 -> 8; matrix products, arithmetic and copies ran while one was open for 7% -> 5% of each run, Pallas kernels for 0% -> 0%
where the time goes in v1:
time: 2300 us; the launch traced here: 2290 us
  waiting for transfers between devices  1320 us (57%)
  matrix products  397 us (17%)
  blocking collectives  239 us (10%)
  local copies, waits for them, and re-layouts  174 us (8%)
  other arithmetic  126 us (5%)
    psum x1, waiting for transfers between devices, local(): lax.psum((expr_grad_local, w_query_grad, b_query_grad, w_key_grad, w_valu...  642 us
    psum x1, waiting for transfers between devices, local(): lax.psum(lax.psum((expr_grad_local, w_query_grad, b_query_grad, w_key_gra...  342 us
    psum x1, blocking collectives, local(): lax.psum(lax.psum((expr_grad_local, w_query_grad, b_query_grad, w_key_gra...  215 us
    all_to_all x1, waiting for transfers between devices, local(): lax.all_to_all(found, ('dp', 'seq'), split_axis=0, concat_axis=0, tiled=T...  140 us
    reduce_scatter x1, waiting for transfers between devices, local(): lax.psum_scatter(grad_v_whole, 'seq', scatter_dimension=1, tiled=True)  74.4 us
    dot_general x24, matrix products, head_scores(): jnp.dot(query_head, key_head.T, preferred_element_type=jnp.float32)  59.4 us
    reduce_scatter x1, waiting for transfers between devices, local(): lax.psum_scatter(grad_k_whole, 'seq', scatter_dimension=1, tiled=True)  50.7 us
    dot_general x1, matrix products, local(): jnp.dot(normed_low, w_up, preferred_element_type=jnp.float32) + b_up  48.7 us
  transfers between devices with their start and end apart: 9, of which 8 were waited for; matrix products, arithmetic and copies ran while one was open for 5% of the time, Pallas kernels for 0%

profile of v1, /device:TPU:0, one launch (start us, length us, event | category | flops | bytes accessed | tf_op | source)
XLA Modules:
  0.0 2288.1 jit_solution(11479150403781075936)
XLA Ops:
  10.3 9.0 reduce-window.14
  19.3 9.0 reduce-window.16
  55.1 17.7 gather_fusion
  83.1 140.1 %all-to-all-done.1 = bf16[32,128,768]{2,1,0:T(8,128)(2,1)} async-done(((bf16[32,128,768]{2,1,0:T(8,128)(2,1)}), bf16[32,128,768]{2,1,0:T(8,128)(2,1)}, u32[]{:S(2)}, u32[]{:S(2)}) %all-to-all-start.1) | async-done | bytes 6291488 | tf_op jit(solution)/shard_map/all_to_all | solution.py:134
  223.3 9.2 gather_fusion.2
  232.4 9.2 gather_fusion.1
  269.0 28.5 %all-gather.5.cloned.1.call-done = bf16[2048,768]{1,0:T(8,128)(2,1)} async-done(((bf16[1024,768]{1,0:T(8,128)(2,1)}), bf16[2048,768]{1,0:T(8,128)(2,1)}) %all-gather.5.cloned.1.call-update) | async-done | bytes 3145744 | tf_op jit(solution)/shard_map/all_gather | solution.py:157
  308.9 35.7 %all-gather.7.cloned.1.call-done = bf16[2048,768]{1,0:T(8,128)(2,1)} async-done(((bf16[1024,768]{1,0:T(8,128)(2,1)}), bf16[2048,768]{1,0:T(8,128)(2,1)}) %all-gather.7.cloned.1.call-update) | async-done | bytes 3145744 | tf_op jit(solution)/shard_map/all_gather | solution.py:158
  356.1 117.5 %while.48 = (s32[]{:T(128)}, bf16[12,1024,64]{1,2,0:T(8,128)(2,1)S(1)}, f32[12,1024]{1,0:T(8,128)}, bf16[12,1024,64]{2,1,0:T(8,128)(2,1)}, bf16[12,2048,64]{2,1,...) while((s32[]{:T(128)}, ...), condition=%wide.region_12.13_spmd.clone, body=%wide.region_9.12_spmd.clone.sunk | while | flops 559948800 | bytes 26810476 | solution.py:46
  478.6 48.7 %multiply_convert_fusion.1 = (bf16[1024,3072]{1,0:T(8,128)(2,1)S(1)}, f32[1024,3072]{1,0:T(8,128)}, f32[1024,3072]{1,0:T(8,128)}) fusion(f32[3072]{0:T(1024)S(1)} %copy-done.50, bf16[768,3072]{1,0:T(8,128)(2,1)S(1)} %bitcast.320, f32[1024,768]{0,1:T(8,128)S(1)} %get-tuple-element.440, f32[768]{0:T(1024)S(1)} %copy-done.55, f32[768]{0:T(1024)S(1)} %copy-done.43, ...), kind=kOutput, calls=%fused_computation.75 | convolution fusion | flops 5043388416 | bytes 39348224 | tf_op jit(solution)/shard_map/dot_general | solution.py:170
  540.1 19.4 convert_reduce_fusion
  559.4 11.4 multiply_reduce_fusion.1
  577.3 225.5 %while.49 = (s32[]{:T(128)}, bf16[12,1024,64]{1,2,0:T(8,128)(2,1)S(1)}, f32[12,2048,64]{1,2,0:T(8,128)}, f32[12,2048,64]{1,2,0:T(8,128)}, bf16[12,1024,64]{2,1,0...) while((s32[]{:T(128)}, ...), condition=%wide.region_23.24_spmd.clone, body=%wide.region_21.23_spmd.clone.sunk | while | flops 1375732736 | bytes 66888828 | solution.py:67
  813.5 8.1 fusion.112
  829.3 50.7 %reduce-scatter.3.cloned.1.call-done = f32[1,1024,768]{1,2,0:T(8,128)} async-done(((f32[1,2048,768]{1,2,0:T(8,128)}), f32[1,1024,768]{1,2,0:T(8,128)}) %reduce-scatter.3.cloned.1.call-update) | async-done | bytes 3145744 | tf_op jit(solution)/shard_map/reduce_scatter | solution.py:214
  885.0 74.4 %reduce-scatter.5.cloned.1.call-done = f32[1,1024,768]{1,2,0:T(8,128)} async-done(((f32[1,2048,768]{1,2,0:T(8,128)}), f32[1,1024,768]{1,2,0:T(8,128)}) %reduce-scatter.5.cloned.1.call-update) | async-done | bytes 3145744 | tf_op jit(solution)/shard_map/reduce_scatter | solution.py:215
  974.6 642.2 %all-reduce.9.cloned.1.call-done = (f32[128,768]{1,0:T(8,128)}, f32[768,768]{1,0:T(8,128)}, f32[768,768]{1,0:T(8,128)}, f32[768,768]{1,0:T(8,128)}, f32[768,768]...) async-done(((f32[128,768]{1,0:T(8,128)}, f32[768,768]{1,0:T(8,128)}, f32[768,768]{1,0:T(8,128)}, f32[768,768]{1,0:T(8,128)}, f32[768,768]{1,0:T(8,128)}, ...) | async-done | bytes 28704784 | tf_op jit(solution)/shard_map/psum | solution.py:252
  1620.6 11.8 scatter_custom_fusion.2
  1632.4 14.9 scatter_fusion.1
  1647.3 8.1 convert_element_type.161
  1667.5 23.2 %all-reduce.2 = (f32[768]{0:T(1024)S(1)}, f32[768]{0:T(1024)S(1)}, f32[768]{0:T(1024)S(1)}, f32[768]{0:T(1024)S(1)}, f32[768]{0:T(1024)S(1)}, /*index=5*/f32[307...) all-reduce(f32[768]{0:T(1024)S(1)} %reduce_sum.262, ...), channel_id=1, replica_groups=mesh['dp'=16,'seq'=2] {'seq'}, use_global_device_ids=true, to_apply=%region_33.34 | all-reduce | flops 9216 | bytes 73728 | tf_op jit(solution)/shard_map/psum | solution.py:252
  1690.7 215.4 %all-reduce = (f32[768]{0:T(1024)}, f32[768]{0:T(1024)}, f32[768]{0:T(1024)}, f32[768]{0:T(1024)}, f32[768]{0:T(1024)}, /*index=5*/f32[3072]{0:T(1024)}, f32[768]{0:T(1024)}, f32[768]{0:T(1024)}, f32[768]{0:T(1024)}) all-reduce(f32[768]{0:T(1024)S(1)} %get-tuple-element.396, ...), channel_id=1, replica_groups=mesh['dp'=16,'seq'=2] {'dp'}, use_global_device_ids=true, to_apply=%region_34.35 | all-reduce | flops 9216 | bytes 73728 | tf_op jit(solution)/shard_map/psum | solution.py:251
  1913.8 342.3 %all-reduce.7.cloned.1.call-done = (f32[128,768]{1,0:T(8,128)}, f32[768,768]{1,0:T(8,128)}, f32[768,768]{1,0:T(8,128)}, f32[768,768]{1,0:T(8,128)}, f32[768,768]...) async-done(((f32[128,768]{1,0:T(8,128)}, f32[768,768]{1,0:T(8,128)}, f32[768,768]{1,0:T(8,128)}, f32[768,768]{1,0:T(8,128)}, f32[768,768]{1,0:T(8,128)}, ...) | async-done | bytes 28704784 | tf_op jit(solution)/shard_map/psum | solution.py:251
  2267.7 9.3 copy.182
  (446 shorter events, 532.8 us)
Async XLA Ops:
  7.2 466.4 %copy-start = (bf16[768,768]{1,0:T(8,128)(2,1)S(1)}, bf16[768,768]{1,0:T(8,128)(2,1)}, u32[]{:S(2)}) copy-start(bf16[768,768]{1,0:T(8,128)(2,1)} %param.43) | copy-start | bytes 3538948
  29.5 53.6 %copy-start.30 = (s32[1024,1]{0,1:T(1,128)}, s32[1024,1]{0,1:T(1,128)S(1)}, u32[]{:S(2)}) copy-start(s32[1024,1]{0,1:T(1,128)S(1)} %compare_select_fusion.2) | copy-start | bytes 12292
  30.0 53.1 %copy-start.40 = (s32[1024,1]{0,1:T(1,128)}, s32[1024,1]{0,1:T(1,128)S(1)}, u32[]{:S(2)}) copy-start(s32[1024,1]{0,1:T(1,128)S(1)} %compare_select_fusion.3) | copy-start | bytes 12292
  34.9 14.9 copy-start.26
  40.6 14.4 all-to-all-start
  55.0 17.8 copy-start.28
  79.4 143.9 %all-to-all-start.1 = ((bf16[32,128,768]{2,1,0:T(8,128)(2,1)}), bf16[32,128,768]{2,1,0:T(8,128)(2,1)}, u32[]{:S(2)}, u32[]{:S(2)}) async-start(bf16[32,128,768]{2,1,0:T(8,128)(2,1)} %broadcast_select_fusion), calls=%async_computation.1 | async-start | bytes 12582912 | tf_op jit(solution)/shard_map/all_to_all | solution.py:134
  83.0 214.5 %all-gather.5.cloned.1.call-start = ((), (), s32[]{:S(2)}) async-start(), calls=%async_computation.7 | async-start | bytes 4718592 | tf_op jit(solution)/shard_map/all_gather | solution.py:157
  253.6 91.0 %all-gather.7.cloned.1.call-start = ((), (), s32[]{:S(2)}) async-start(), calls=%async_computation.8 | async-start | bytes 4718592 | tf_op jit(solution)/shard_map/all_gather | solution.py:158
  257.7 622.4 %reduce-scatter.3.cloned.1.call-start = ((), (), s32[]{:S(2)}) async-start(), calls=%async_computation.5 | async-start | bytes 9437184 | tf_op jit(solution)/shard_map/reduce_scatter | solution.py:214
  356.1 117.6 %copy-start.53 = (f32[768]{0:T(1024)S(1)}, f32[768]{0:T(1024)}, u32[]{:S(2)}) copy-start(f32[768]{0:T(1024)} %param.44) | copy-start | bytes 9220
  473.7 53.7 %slice-start.3 = ((s8[4718592]{0:T(1024)(128)(4,1)}), s8[4194304]{0:T(1024)(128)(4,1)S(1)}, s32[]{:S(2)}) async-start(s8[4718592]{0:T(1024)(128)(4,1)} %bitcast.317), calls=%async_computation.14 | async-start | bytes 8388608
  477.7 49.6 %copy-start.7 = (f32[1024,768]{0,1:T(8,128)}, f32[1024,768]{0,1:T(8,128)S(1)}, u32[]{:S(2)}) copy-start(f32[1024,768]{0,1:T(8,128)S(1)} %get-tuple-element.440) | copy-start | bytes 9437188
  478.6 48.8 %slice-start.4 = ((s8[4718592]{0:T(1024)(128)(4,1)}), s8[524288]{0:T(1024)(128)(4,1)S(1)}, s32[]{:S(2)}) async-start(s8[4718592]{0:T(1024)(128)(4,1)} %bitcast.317), calls=%async_computation.15 | async-start | bytes 1048576
  478.6 48.8 %copy-start.54 = (f32[768]{0:T(1024)S(1)}, f32[768]{0:T(1024)}, u32[]{:S(2)}) copy-start(f32[768]{0:T(1024)} %param.50) | copy-start | bytes 9220
  802.8 156.6 %reduce-scatter.5.cloned.1.call-start = ((), (), s32[]{:S(2)}) async-start(), calls=%async_computation.6 | async-start | bytes 9437184 | tf_op jit(solution)/shard_map/reduce_scatter | solution.py:215
  803.4 813.4 %all-reduce.9.cloned.1.call-start = ((), (), s32[]{:S(2)}) async-start(), calls=%async_computation.10 | async-start | bytes 57409536 | tf_op jit(solution)/shard_map/psum | solution.py:252
  821.6 58.4 %copy-start.49 = (bf16[768,768]{1,0:T(8,128)(2,1)S(1)}, bf16[768,768]{1,0:T(8,128)(2,1)}, u32[]{:S(2)}) copy-start(bf16[768,768]{1,0:T(8,128)(2,1)} %param.40) | copy-start | bytes 3538948
  829.3 130.1 %copy-start.25 = (bf16[768,768]{1,0:T(8,128)(2,1)S(1)}, bf16[768,768]{1,0:T(8,128)(2,1)}, u32[]{:S(2)}) copy-start(bf16[768,768]{1,0:T(8,128)(2,1)} %param.41) | copy-start | bytes 3538948
  829.3 130.1 %copy-start.34 = (f32[1024]{0:T(1024)S(1)}, f32[1024]{0:T(1024)}, u32[]{:S(2)}) copy-start(f32[1024]{0:T(1024)} %copy-done.33) | copy-start | bytes 12292
  885.0 80.6 %copy-start.36 = (s32[1,1024]{1,0:T(1,128)S(1)}, s32[1,1024]{1,0:T(1,128)}, u32[]{:S(2)}) copy-start(s32[1,1024]{1,0:T(1,128)} %param.32) | copy-start | bytes 12292
  974.6 1281.5 %all-reduce.7.cloned.1.call-start = ((), (), s32[]{:S(2)}) async-start(), calls=%async_computation.9 | async-start | bytes 57409536 | tf_op jit(solution)/shard_map/psum | solution.py:251
  1620.6 11.8 copy-start.31
  1655.4 250.7 %all-to-all-start.2 = ((bf16[32,128,768]{2,1,0:T(8,128)(2,1)}), bf16[32,128,768]{2,1,0:T(8,128)(2,1)}, u32[]{:S(2)}, u32[]{:S(2)}) async-start(bf16[32,128,768]{2,1,0:T(8,128)(2,1)} %bitcast.274), calls=%async_computation.4 | async-start | bytes 12582912 | tf_op jit(solution)/shard_map/all_to_all | solution.py:241
  (54 other events, 241.0 us)
Sparse Core Ops, SparseCore 0:
  253.7 43.7 all-gather.4
  299.6 44.9 all-gather.6
  803.0 77.0 reduce-scatter.2
  882.3 77.0 reduce-scatter.4
  974.7 642.0 all-reduce.8
  1622.5 633.5 all-reduce.6
